TPU v7x, 32 devices: a whole 2x2x4 slice. The times are simulated.
32 devices in a mesh: dp: 8 (over y, x, core), seq: 4 (over z).
Axes of the slice: x: 2, y: 2, z: 4, core: 2. Of those that a mesh axis runs over, the one named last changes fastest.
Arguments:
- queries: bfloat16 [16, 256, 5120], P('dp', 'seq'), may hold values from -50 to 50
- key_rows: bfloat16 [16, 256, 1024], P('dp', 'seq'), may hold values from -6 to 6
- value_rows: bfloat16 [16, 256, 1024], P('dp', 'seq'), may hold values from -6 to 6
- cotangent: bfloat16 [16, 256, 5120], P('dp', 'seq'), may hold values from -6 to 6
- episodes: int32 [16, 256], P('dp', 'seq'), may hold values from 0 to 7, never falling along the last dimension, each value on 1 to 170 neighbouring positions
- send_slot: int32 [8], P('dp'), may hold values from 0 to 1
- swap_mask: int32 [1], replicated, may hold values from 1 to 7
Outputs:
- grad_queries: bfloat16 [16, 256, 5120], P('dp', 'seq')
- grad_keys: bfloat16 [16, 256, 1024], P('dp', 'seq')
- grad_values: bfloat16 [16, 256, 1024], P('dp', 'seq')
Inputs may be any that keep to these rules, and one draw needn't show every extreme that they name: `episodes`: episode ids never fall along a span.
All inputs are finite; a program needn't handle non-finite values.
Results may differ from a plain program's by a relative error of at most 0.0055.
Values may be sent and summed in bfloat16 or wider, within the bound.
A program may use at most 64 MiB of HBM per device.

v0:
```python
import functools

import jax
import jax.numpy as jnp
from jax import lax
from jax.experimental import pallas as pl
from jax.experimental.pallas import tpu as pltpu
from jax.sharding import PartitionSpec as P

DH = 128
HP = 2
LAG = 2
AHEAD = 2
OWN = 1
MESH = pl.DeviceIdType.MESH
NT = (((1,), (1,)), ((), ()))
NN = (((1,), (0,)), ((), ()))
TN = (((0,), (0,)), ((), ()))


def dot(a, b, dims):
    return lax.dot_general(a, b, dims, preferred_element_type=jnp.float32)


def kernel(
    n, ndp, mask, send_ref, ep_ref, q_hbm, k_hbm, v_hbm, do_hbm,
    gq_out, gk_out, gv_out,
    q_ref, k_ref, v_ref, do_ref, load_sem, keep_sem, kvbuf, epbuf, allow, gpart, gown, grecv, tq, tk, tv,
    up_send, up_recv, ep_send, ep_recv, down_send, down_recv, trade_send, trade_recv,
):
    r = lax.axis_index("dp")
    s = lax.axis_index("seq")
    rows = q_ref.shape[1]
    heads = k_ref.shape[2] // DH
    groups = q_ref.shape[2] // k_ref.shape[2]
    per = heads // HP
    pieces = 2 * per
    keys = n * rows
    wide = groups * rows
    scaling = 1.0 / jnp.sqrt(jnp.float32(DH))
    partner = r
    for b in range(ndp.bit_length() - 1):
        if (mask >> b) & 1:
            partner = partner + (1 << b) * (1 - 2 * ((r // (1 << b)) % 2))
    handed = send_ref[0]
    most = 2 * n * rows // 3

    def first(d):
        return min(max(0, d * rows - most + 1) // 16 * 16, rows)

    reach = [d for d in range(1, n) if first(d) < rows]
    own = pl.ds(pl.multiple_of(s * rows, rows), rows)

    def slot(c):
        return handed + c * (1 - 2 * handed)

    barrier = pltpu.get_barrier_semaphore()
    for d in range(1, n):
        pl.semaphore_signal(barrier, inc=1, device_id=(r, (s + d) % n), device_id_type=MESH)
    pl.semaphore_signal(barrier, inc=1, device_id=(partner, s), device_id_type=MESH)
    loads = [
        pltpu.make_async_copy(src, dst, load_sem.at[i])
        for i, (src, dst) in enumerate(
            ((k_hbm, k_ref), (v_hbm, v_ref), (q_hbm, q_ref), (do_hbm, do_ref))
        )
    ]
    for load in loads:
        load.start()
    loads[0].wait()
    loads[1].wait()

    for c in range(2):
        epbuf[s, c:c + 1, 0:rows] = jnp.where(
            slot(c) == 0, ep_ref[0:1, :], ep_ref[1:2, :]
        )
        for g in range(heads):
            kvbuf[c, g, own, 0:DH] = k_ref[slot(c), :, g * DH:(g + 1) * DH]
            kvbuf[c, g, own, DH:2 * DH] = v_ref[slot(c), :, g * DH:(g + 1) * DH]
    pl.semaphore_wait(barrier, n)

    def chunk(t, low=0):
        return pl.ds(pl.multiple_of(t * rows + low, 16), rows - low)

    def up(p, t, d):
        part = kvbuf.at[p // per, pl.ds((p % per) * HP, HP), chunk(t, first(d)), :]
        return pltpu.make_async_remote_copy(
            src_ref=part, dst_ref=part,
            send_sem=up_send.at[p, t], recv_sem=up_recv.at[p, t],
            device_id=(r, (s + 1) % n), device_id_type=MESH,
        )

    def ep_copy(src, dst):
        return pltpu.make_async_remote_copy(
            src_ref=epbuf.at[src], dst_ref=epbuf.at[src],
            send_sem=ep_send.at[dst], recv_sem=ep_recv.at[src],
            device_id=(r, dst), device_id_type=MESH,
        )

    def down(p, t, d):
        c, g = p // per, (p % per) * HP
        part = (c, pl.ds(g, HP), chunk(t, first(d)))
        return pltpu.make_async_remote_copy(
            src_ref=gpart.at[part], dst_ref=grecv.at[part],
            send_sem=down_send.at[p, t], recv_sem=down_recv.at[p, t],
            device_id=(r, (s + n - 1) % n), device_id_type=MESH,
        )

    def trade(which, p, buf, out, width):
        cols = pl.ds(pl.multiple_of(p * HP * width, HP * width), HP * width)
        return pltpu.make_async_remote_copy(
            src_ref=buf.at[0, :, cols], dst_ref=out.at[1, :, cols],
            send_sem=trade_send.at[which, p], recv_sem=trade_recv.at[which, p],
            device_id=(partner, s), device_id_type=MESH,
        )

    def keep(which, p, buf, out, width):
        cols = pl.ds(pl.multiple_of(p * HP * width, HP * width), HP * width)
        return pltpu.make_async_copy(
            buf.at[1, :, cols], out.at[0, :, cols], keep_sem.at[which, p]
        )

    for t in range(n - 1, 0, -1):
        @pl.when(t > s)
        def _(t=t):
            ep_copy(s, t).start()

    def send_own(p):
        @pl.when((s < n - 1) & (p < pieces))
        def _():
            up(p, s, 1).start()

    for p in range(OWN):
        send_own(p)

    def clear(t, size):
        def one(i, carry):
            kvbuf[i // heads, i % heads, pl.ds(pl.multiple_of(t * rows, rows), size), :] = (
                jnp.zeros((size, 2 * DH), jnp.bfloat16)
            )
            return carry

        lax.fori_loop(0, 2 * heads, one, 0)

    for t in range(n):
        @pl.when(t > s)
        def _(t=t):
            epbuf[t, :, :] = jnp.full((8, DH), -1, jnp.int32)
            clear(t, rows)
    for d in range(1, n):
        if first(d) > 0:
            @pl.when(s >= d)
            def _(d=d):
                clear(s - d, first(d))

    for t in range(n - 1):
        @pl.when(t < s)
        def _(t=t):
            ep_copy(t, s).wait_recv()

    eye = lax.broadcasted_iota(jnp.int32, (rows, DH), 0) == lax.broadcasted_iota(
        jnp.int32, (rows, DH), 1
    )
    for c in range(2):
        mine = epbuf[s, c:c + 1, 0:rows]
        mine = jnp.concatenate([mine] * groups, axis=1)
        pos_q = jnp.concatenate(
            [s * rows + lax.broadcasted_iota(jnp.int32, (rows, rows), 1)] * groups, axis=1
        )
        for t in range(n):
            line = epbuf[t, c:c + 1, :]
            column = jnp.sum(jnp.where(eye, line, 0), axis=1, keepdims=True)
            pos_k = t * rows + lax.broadcasted_iota(jnp.int32, (rows, wide), 0)
            seen = jnp.where(pos_k <= pos_q, 1.0, 0.0) * jnp.where(column == mine, 1.0, 0.0)
            allow[c, t * rows:(t + 1) * rows, :] = seen

    loads[2].wait()
    loads[3].wait()

    def compute(p):
        c, g0 = p // per, (p % per) * HP
        at = slot(c)
        for j in range(HP):
            g = g0 + j

            def stack(ref):
                return jnp.concatenate(
                    [
                        ref[at, :, pl.ds(pl.multiple_of((g * groups + i) * DH, DH), DH)]
                        for i in range(groups)
                    ],
                    axis=0,
                )

            q = stack(q_ref)
            do = stack(do_ref)
            key = kvbuf[c, g, :, 0:DH]
            value = kvbuf[c, g, :, DH:2 * DH]
            scores = jnp.where(allow[c] > 0.5, dot(key, q, NT) * scaling, jnp.float32(-1e30))
            top = jnp.max(scores, axis=0, keepdims=True)
            expo = jnp.exp(scores - top)
            probs = expo * (1.0 / jnp.sum(expo, axis=0, keepdims=True))
            dprobs = dot(value, do, NT)
            delta = jnp.sum(probs * dprobs, axis=0, keepdims=True)
            dscores = (probs * (dprobs - delta)).astype(jnp.bfloat16)
            gk = dot(dscores, q, NN)
            gv = dot(probs.astype(jnp.bfloat16), do, NN)
            gown[c, g, :, 0:DH] = gk
            gown[c, g, :, DH:2 * DH] = gv
            gq = (dot(dscores, key, TN) * scaling).astype(jnp.bfloat16)
            for i in range(groups):
                cols = pl.ds(pl.multiple_of((g * groups + i) * DH, DH), DH)
                tq[c, :, cols] = gq[i * rows:(i + 1) * rows]

        @pl.when(c == 0)
        def _():
            trade(0, p, tq, gq_out, groups * DH).start()

        @pl.when(c == 1)
        def _():
            keep(0, p - per, tq, gq_out, groups * DH).start()

    def forward(p):
        for d in reach:
            @pl.when(s >= d)
            def _(d=d):
                up(p, s - d, d).wait_recv()
                if d + 1 in reach:
                    @pl.when(s < n - 1)
                    def _():
                        up(p, s - d, d + 1).start()

    def finish(p):
        c, g0 = p // per, (p % per) * HP
        for d in reversed([0] + reach):
            if d + 1 in reach:
                @pl.when((s >= d) & (s < n - 1))
                def _(d=d):
                    part = (c, pl.ds(g0, HP), chunk(s - d, first(d + 1)))
                    down(p, s - d, d + 1).wait_recv()
                    gown[part] += grecv[part].astype(jnp.float32)
            if d > 0:
                @pl.when(s >= d)
                def _(d=d):
                    part = (c, pl.ds(g0, HP), chunk(s - d, first(d)))
                    gpart[part] = gown[part].astype(jnp.bfloat16)
                    down(p, s - d, d).start()
        for j in range(HP):
            g = g0 + j
            cols = pl.ds(pl.multiple_of(g * DH, DH), DH)
            gk = (gown[c, g, own, 0:DH] * scaling).astype(jnp.bfloat16)
            gv = gown[c, g, own, DH:2 * DH].astype(jnp.bfloat16)

            tk[c, :, cols] = gk
            tv[c, :, cols] = gv

        @pl.when(c == 0)
        def _():
            trade(1, p, tk, gk_out, DH).start()
            trade(2, p, tv, gv_out, DH).start()

        @pl.when(c == 1)
        def _():
            keep(1, p - per, tk, gk_out, DH).start()
            keep(2, p - per, tv, gv_out, DH).start()

    behind = jnp.where(s == n - 1, 0, AHEAD)
    late = behind + LAG * (n - 1 - s)

    def step(i, carry):
        send_own(i + OWN)

        @pl.when(i < pieces)
        def _():
            forward(i)

        @pl.when((i >= behind) & (i < pieces + behind))
        def _():
            compute(i - behind)

        @pl.when((i >= late) & (i < pieces + late))
        def _():
            finish(i - late)
        return carry

    lax.fori_loop(0, pieces + AHEAD + LAG * (n - 1), step, 0)

    def drain(p, carry):
        for d in reach:
            @pl.when((s >= d - 1) & (s < n - 1))
            def _(d=d):
                up(p, s - d + 1, d).wait_send()

            @pl.when(s >= d)
            def _(d=d):
                down(p, s - d, d).wait_send()
        return carry

    lax.fori_loop(0, pieces, drain, 0)
    for t in range(1, n):
        @pl.when(t > s)
        def _(t=t):
            ep_copy(s, t).wait_send()

    def drain_trade(p, carry):
        trade(0, p, tq, gq_out, groups * DH).wait()
        trade(1, p, tk, gk_out, DH).wait()
        trade(2, p, tv, gv_out, DH).wait()
        keep(0, p, tq, gq_out, groups * DH).wait()
        keep(1, p, tk, gk_out, DH).wait()
        keep(2, p, tv, gv_out, DH).wait()
        return carry

    lax.fori_loop(0, per, drain_trade, 0)


def call(n, ndp, mask, send_slot, episodes, queries, key_rows, value_rows, cotangent):
    rows = queries.shape[1]
    heads = key_rows.shape[2] // DH
    groups = queries.shape[2] // key_rows.shape[2]
    pieces = 2 * heads // HP
    vmem = pl.BlockSpec(memory_space=pltpu.VMEM)
    dma = pltpu.SemaphoreType.DMA
    return pl.pallas_call(
        functools.partial(kernel, n, ndp, mask),
        out_shape=[
            jax.ShapeDtypeStruct(x.shape, x.dtype) for x in (queries, key_rows, value_rows)
        ],
        in_specs=[pl.BlockSpec(memory_space=pltpu.SMEM), vmem]
        + [pl.BlockSpec(memory_space=pl.ANY)] * 4,
        out_specs=[pl.BlockSpec(memory_space=pl.ANY)] * 3,
        scratch_shapes=[
            pltpu.VMEM(queries.shape, jnp.bfloat16),
            pltpu.VMEM(key_rows.shape, jnp.bfloat16),
            pltpu.VMEM(value_rows.shape, jnp.bfloat16),
            pltpu.VMEM(cotangent.shape, jnp.bfloat16),
            dma((4,)),
            dma((3, pieces // 2)),
            pltpu.VMEM((2, heads, n * rows, 2 * DH), jnp.bfloat16),
            pltpu.VMEM((n, 8, DH), jnp.int32),
            pltpu.VMEM((2, n * rows, groups * rows), jnp.float32),
            pltpu.VMEM((2, heads, n * rows, 2 * DH), jnp.bfloat16),
            pltpu.VMEM((2, heads, n * rows, 2 * DH), jnp.float32),
            pltpu.VMEM((2, heads, n * rows, 2 * DH), jnp.bfloat16),
            pltpu.VMEM(queries.shape, jnp.bfloat16),
            pltpu.VMEM(key_rows.shape, jnp.bfloat16),
            pltpu.VMEM(value_rows.shape, jnp.bfloat16),
            dma((pieces, n)),
            dma((pieces, n)),
            dma((n,)),
            dma((n,)),
            dma((pieces, n)),
            dma((pieces, n)),
            dma((3, pieces // 2)),
            dma((3, pieces // 2)),
        ],
        compiler_params=pltpu.CompilerParams(collective_id=mask, has_side_effects=True),
    )(send_slot, episodes, queries, key_rows, value_rows, cotangent)


def solution(mesh):
    n, ndp = mesh.shape["seq"], mesh.shape["dp"]

    def per_device(queries, key_rows, value_rows, cotangent, episodes, send_slot, swap_mask):
        return tuple(lax.switch(
            swap_mask[0] - 1,
            [functools.partial(call, n, ndp, mask) for mask in range(1, ndp)],
            send_slot, episodes, queries, key_rows, value_rows, cotangent,
        ))

    in_specs = (
        P("dp", "seq", None),
        P("dp", "seq", None),
        P("dp", "seq", None),
        P("dp", "seq", None),
        P("dp", "seq"),
        P("dp"),
        P(),
    )
    out_specs = (P("dp", "seq", None), P("dp", "seq", None), P("dp", "seq", None))
    return jax.shard_map(
        per_device, mesh=mesh, in_specs=in_specs, out_specs=out_specs, check_vma=False
    )
```

profile of v0, /device:TPU:0, one launch (start us, length us, event | category | flops | bytes accessed | tf_op | source)
XLA Modules:
  0.0 59.8 jit_solution(10058030931542527177)
XLA Ops:
  1.3 56.0 %conditional.1 = ((bf16[2,64,5120]{2,1,0:T(8,128)(2,1)S(1)}, bf16[2,64,1024]{2,1,0:T(8,128)(2,1)S(1)}, bf16[2,64,1024]{2,1,0:T(8,128)(2,1)S(1)})) conditional(s32[]{:T(128)} %bitcast, (s32[1]{0:T(128)}, s32[2,64]{1,0:T(2,128)}, bf16[2,64,5120]{2,1,0:T(8,128)(2,1)}, bf16[2,64,1024]{2,1,0:T(8,128)(2,1)}, ...), branch_computations={%region_0.0_spmd, %region_1.0_spmd, %region_2.0_spmd, %region_3.0_... | conditional | bytes 8 | solution.py:364
  1.3 56.0 %branch_2_fun.1 = (bf16[2,64,5120]{2,1,0:T(8,128)(2,1)S(1)}, bf16[2,64,1024]{2,1,0:T(8,128)(2,1)S(1)}, bf16[2,64,1024]{2,1,0:T(8,128)(2,1)S(1)}) custom-call(s32[1]{0:T(128)} %get-tuple-element.96.send_ref, s32[2,64]{1,0:T(2,128)} %get-tuple-element.97.ep_ref, bf16[2,64,5120]{2,1,0:T(8,128)(2,1)} %get-tuple-element.98.q_hbm, ...), custom_call_target="tpu_custom_call" | custom-call | tf_op jit(solution)/shard_map/cond/branch_2_fun/pallas_call | solution.py:323
  57.3 1.1 %copy.56 = bf16[2,64,5120]{2,1,0:T(8,128)(2,1)} copy(bf16[2,64,5120]{2,1,0:T(8,128)(2,1)S(1)} %get-tuple-element.177) | data formatting | bytes 2621440
  58.3 0.7 %copy.57 = bf16[2,64,1024]{2,1,0:T(8,128)(2,1)} copy(bf16[2,64,1024]{2,1,0:T(8,128)(2,1)S(1)} %get-tuple-element.178) | data formatting | bytes 524288
  59.1 0.7 %copy.58 = bf16[2,64,1024]{2,1,0:T(8,128)(2,1)} copy(bf16[2,64,1024]{2,1,0:T(8,128)(2,1)S(1)} %get-tuple-element.179) | data formatting | bytes 524288
where the time goes:
time: 59.9 us; the launch traced here: 59.8 us
  Pallas kernels  56 us (93%)
  local copies, waits for them, and re-layouts  2.46 us (4%)
  between operations  1.29 us (2%)
    pallas_call x1, Pallas kernels, call(): pl.pallas_call(functools.partial(kernel, n, ndp, mask), out_shape=[jax.Sh...  56 us
    unnamed x3, local copies, waits for them, and re-layouts  2.46 us

commit v1 on v0

--- a/solution.py
+++ b/solution.py
@@ -23,9 +23,9 @@
 
 
 def kernel(
-    n, ndp, mask, send_ref, ep_ref, q_hbm, k_hbm, v_hbm, do_hbm,
+    n, ndp, mask, send_hbm, ep_hbm, q_hbm, k_hbm, v_hbm, do_hbm,
     gq_out, gk_out, gv_out,
-    q_ref, k_ref, v_ref, do_ref, load_sem, keep_sem, kvbuf, epbuf, allow, gpart, gown, grecv, tq, tk, tv,
+    send_ref, ep_ref, q_ref, k_ref, v_ref, do_ref, load_sem, keep_sem, kvbuf, epbuf, allow, gpart, gown, grecv, tq, tk, tv,
     up_send, up_recv, ep_send, ep_recv, down_send, down_recv, trade_send, trade_recv,
 ):
     r = lax.axis_index("dp")
@@ -42,7 +42,6 @@
     for b in range(ndp.bit_length() - 1):
         if (mask >> b) & 1:
             partner = partner + (1 << b) * (1 - 2 * ((r // (1 << b)) % 2))
-    handed = send_ref[0]
     most = 2 * n * rows // 3
 
     def first(d):
@@ -50,9 +49,6 @@
 
     reach = [d for d in range(1, n) if first(d) < rows]
     own = pl.ds(pl.multiple_of(s * rows, rows), rows)
-
-    def slot(c):
-        return handed + c * (1 - 2 * handed)
 
     barrier = pltpu.get_barrier_semaphore()
     for d in range(1, n):
@@ -61,13 +57,20 @@
     loads = [
         pltpu.make_async_copy(src, dst, load_sem.at[i])
         for i, (src, dst) in enumerate(
-            ((k_hbm, k_ref), (v_hbm, v_ref), (q_hbm, q_ref), (do_hbm, do_ref))
+            (
+                (send_hbm, send_ref), (ep_hbm, ep_ref), (k_hbm, k_ref), (v_hbm, v_ref),
+                (q_hbm, q_ref), (do_hbm, do_ref),
+            )
         )
     ]
-    for load in loads:
+    for load in loads[:4]:
         load.start()
-    loads[0].wait()
-    loads[1].wait()
+    for load in loads[:4]:
+        load.wait()
+    handed = send_ref[0]
+
+    def slot(c):
+        return handed + c * (1 - 2 * handed)
 
     for c in range(2):
         epbuf[s, c:c + 1, 0:rows] = jnp.where(
@@ -76,6 +79,8 @@
         for g in range(heads):
             kvbuf[c, g, own, 0:DH] = k_ref[slot(c), :, g * DH:(g + 1) * DH]
             kvbuf[c, g, own, DH:2 * DH] = v_ref[slot(c), :, g * DH:(g + 1) * DH]
+    for load in loads[4:]:
+        load.start()
     pl.semaphore_wait(barrier, n)
 
     def chunk(t, low=0):
@@ -173,8 +178,8 @@
             seen = jnp.where(pos_k <= pos_q, 1.0, 0.0) * jnp.where(column == mine, 1.0, 0.0)
             allow[c, t * rows:(t + 1) * rows, :] = seen
 
-    loads[2].wait()
-    loads[3].wait()
+    loads[4].wait()
+    loads[5].wait()
 
     def compute(p):
         c, g0 = p // per, (p % per) * HP
@@ -318,22 +323,22 @@
     heads = key_rows.shape[2] // DH
     groups = queries.shape[2] // key_rows.shape[2]
     pieces = 2 * heads // HP
-    vmem = pl.BlockSpec(memory_space=pltpu.VMEM)
     dma = pltpu.SemaphoreType.DMA
     return pl.pallas_call(
         functools.partial(kernel, n, ndp, mask),
         out_shape=[
             jax.ShapeDtypeStruct(x.shape, x.dtype) for x in (queries, key_rows, value_rows)
         ],
-        in_specs=[pl.BlockSpec(memory_space=pltpu.SMEM), vmem]
-        + [pl.BlockSpec(memory_space=pl.ANY)] * 4,
+        in_specs=[pl.BlockSpec(memory_space=pl.ANY)] * 6,
         out_specs=[pl.BlockSpec(memory_space=pl.ANY)] * 3,
         scratch_shapes=[
+            pltpu.SMEM(send_slot.shape, jnp.int32),
+            pltpu.VMEM(episodes.shape, jnp.int32),
             pltpu.VMEM(queries.shape, jnp.bfloat16),
             pltpu.VMEM(key_rows.shape, jnp.bfloat16),
             pltpu.VMEM(value_rows.shape, jnp.bfloat16),
             pltpu.VMEM(cotangent.shape, jnp.bfloat16),
-            dma((4,)),
+            dma((6,)),
             dma((3, pieces // 2)),
             pltpu.VMEM((2, heads, n * rows, 2 * DH), jnp.bfloat16),
             pltpu.VMEM((n, 8, DH), jnp.int32),
@@ -357,15 +362,36 @@
     )(send_slot, episodes, queries, key_rows, value_rows, cotangent)
 
 
+def emit(a_ref, b_ref, c_ref, a_out, b_out, c_out, sems):
+    copies = [
+        pltpu.make_async_copy(src, dst, sems.at[i])
+        for i, (src, dst) in enumerate(((a_ref, a_out), (b_ref, b_out), (c_ref, c_out)))
+    ]
+    for copy in copies:
+        copy.start()
+    for copy in copies:
+        copy.wait()
+
+
+def deliver(*grads):
+    return pl.pallas_call(
+        emit,
+        out_shape=[jax.ShapeDtypeStruct(x.shape, x.dtype) for x in grads],
+        in_specs=[pl.BlockSpec(memory_space=pl.ANY)] * 3,
+        out_specs=[pl.BlockSpec(memory_space=pl.ANY)] * 3,
+        scratch_shapes=[pltpu.SemaphoreType.DMA((3,))],
+    )(*grads)
+
+
 def solution(mesh):
     n, ndp = mesh.shape["seq"], mesh.shape["dp"]
 
     def per_device(queries, key_rows, value_rows, cotangent, episodes, send_slot, swap_mask):
-        return tuple(lax.switch(
+        return tuple(deliver(*lax.switch(
             swap_mask[0] - 1,
             [functools.partial(call, n, ndp, mask) for mask in range(1, ndp)],
             send_slot, episodes, queries, key_rows, value_rows, cotangent,
-        ))
+        )))
 
     in_specs = (
         P("dp", "seq", None),

time: 59.9 us -> 58.1 us (0.970)
  local copies, waits for them, and re-layouts: 2.46 us -> 0 us
  Pallas kernels: 56 us -> 56.6 us
    unnamed x3 -> x0, local copies, waits for them, and re-layouts: 2.46 us -> none
    pallas_call x0 -> x1, Pallas kernels: none -> 1.25 us  [deliver(): pl.pallas_call(emit, out_shape=[jax.ShapeDtypeStruct(x.shape, x.dtype) fo...]
    pallas_call x1, Pallas kernels: 56 us -> 55.3 us  [call(): pl.pallas_call(functools.partial(kernel, n, ndp, mask), out_shape=[jax.Sh...]
where the time goes in v1:
time: 58.1 us; the launch traced here: 57.9 us
  Pallas kernels  56.6 us (97%)
  between operations  1.29 us (2%)
    pallas_call x1, Pallas kernels, call(): pl.pallas_call(functools.partial(kernel, n, ndp, mask), out_shape=[jax.Sh...  55.3 us
    pallas_call x1, Pallas kernels, deliver(): pl.pallas_call(emit, out_shape=[jax.ShapeDtypeStruct(x.shape, x.dtype) fo...  1.25 us

profile of v1, /device:TPU:0, one launch (start us, length us, event | category | flops | bytes accessed | tf_op | source)
XLA Modules:
  0.0 57.9 jit_solution(10329317573261545424)
XLA Ops:
  1.3 55.4 %conditional.1 = ((bf16[2,64,5120]{2,1,0:T(8,128)(2,1)S(1)}, bf16[2,64,1024]{2,1,0:T(8,128)(2,1)S(1)}, bf16[2,64,1024]{2,1,0:T(8,128)(2,1)S(1)})) conditional(s32[]{:T(128)} %bitcast, (s32[1]{0:T(128)}, s32[2,64]{1,0:T(2,128)}, bf16[2,64,5120]{2,1,0:T(8,128)(2,1)}, bf16[2,64,1024]{2,1,0:T(8,128)(2,1)}, ...), branch_computations={%region_0.0_spmd, %region_1.0_spmd, %region_2.0_spmd, %region_3.0_... | conditional | bytes 8 | solution.py:390
  1.3 55.3 %branch_5_fun.1 = (bf16[2,64,5120]{2,1,0:T(8,128)(2,1)S(1)}, bf16[2,64,1024]{2,1,0:T(8,128)(2,1)S(1)}, bf16[2,64,1024]{2,1,0:T(8,128)(2,1)S(1)}) custom-call(s32[1]{0:T(128)} %get-tuple-element.114.send_hbm, s32[2,64]{1,0:T(2,128)} %get-tuple-element.115.ep_hbm, bf16[2,64,5120]{2,1,0:T(8,128)(2,1)} %get-tuple-element.116.q_hbm, ...), custom_call_target="tpu_custom_call" | custom-call | tf_op jit(solution)/shard_map/cond/branch_5_fun/pallas_call | solution.py:327
  56.7 1.2 %shard_map.94 = (bf16[2,64,5120]{2,1,0:T(8,128)(2,1)}, bf16[2,64,1024]{2,1,0:T(8,128)(2,1)}, bf16[2,64,1024]{2,1,0:T(8,128)(2,1)}) custom-call(bf16[2,64,5120]{2,1,0:T(8,128)(2,1)S(1)} %get-tuple-element.132.a_ref, bf16[2,64,1024]{2,1,0:T(8,128)(2,1)S(1)} %get-tuple-element.133.b_ref, bf16[2,64,1024]{2,1,0:T(8,128)(2,1)S(1)} %get-tuple-element.134.c_ref), custom_call_target="tpu_custom_call" | custom-call | tf_op jit(solution)/shard_map/pallas_call | solution.py:377
